TPU v7x, 512 devices: a whole 4x8x8 slice. The times are simulated.
512 devices in a mesh: blk: 64 (over x, z_hi, y), grp: 8 (over z_lo, core).
Axes of the slice: x: 4, y: 8, z: 8 (z_hi: 2, z_lo: 4; z = z_hi * 4 + z_lo), core: 2. Of those that a mesh axis runs over, the one named last changes fastest.
Arguments:
- excitation: bfloat16 [128, 1024, 256], P('blk'), may hold values from -6 to 6
- inverse_self: bfloat16 [128, 1024, 1024], P('blk', 'grp'), may hold values from -0.1875 to 0.1875
- coupling: bfloat16 [128, 4, 1024, 1024], P('blk', None, 'grp'), may hold values from -0.1875 to 0.1875
- neighbour_mask: int32 [128, 4], P('blk'), may hold values 0 or 1
- sketch: float32 [5, 256, 32], replicated, may hold values from -6 to 6
Outputs:
- bases: float32 [128, 1024, 32], P('blk', 'grp')
- reduced_coupling: float32 [128, 4, 32, 32], P('blk')
- reduced_excitation: float32 [128, 32, 256], P('blk')
Inputs may be any that keep to these rules, and one draw needn't show every extreme that they name: `neighbour_mask`: 1 where the block at that slot's offset adds secondary currents, 0 where it does not; slots pointing outside the array add nothing in any case.
All inputs are finite; a program needn't handle non-finite values.
Results may differ from a plain program's by a relative error of at most 0.0003.
Values sent between devices are 32-bit elements; how exact they have to be, the bound alone decides.
No kernel may reach another device: no remote copies, remote signals or barrier semaphores. Data moves between devices by JAX's collectives and lax.ppermute only.
A program may use at most 64 MiB of HBM per device.

v0:
```python
import math
import jax
import jax.numpy as jnp
from jax import lax
from jax.sharding import PartitionSpec as P

neighbour_offsets = (-2, -1, 1, 2)


def extended(array, sides, width):
    for axis, dim in sides:
        size, length = (lax.axis_size(axis), array.shape[dim])
        up = [(i, (i + 1) % size) for i in range(size - 1)]
        down = [(j, i) for i, j in up]
        last = lax.slice_in_dim(array, length - width, length, axis=dim)
        initial = lax.slice_in_dim(array, 0, width, axis=dim)
        before = lax.ppermute(last, axis, up)
        after = lax.ppermute(initial, axis, down)
        array = jnp.concatenate([before, array, after], axis=dim)
    return array


def exact_einsum(form, left, right):
    return jnp.einsum(
        form, left, right, precision=lax.Precision.HIGHEST, preferred_element_type=jnp.float32
    )


def shards(excitation, inverse_self, coupling, neighbour_mask, sketch):
    blocks, unknowns, columns = excitation.shape
    shard_rows = inverse_self.shape[1]
    retained = sketch.shape[2]
    row_start = lax.axis_index("grp") * shard_rows
    own_excitation = lax.dynamic_slice_in_dim(excitation, row_start, shard_rows, 1)
    primary = jnp.einsum(
        "bnm,bmp->bnp", inverse_self, excitation, preferred_element_type=jnp.float32
    )
    weights_mask = neighbour_mask.astype(jnp.float32)
    own_whole = lax.all_gather(primary, "grp", axis=1, tiled=True)
    nearby = extended(own_whole, (("blk", 0),), 2)
    sources = jnp.zeros((blocks, shard_rows, retained), jnp.float32)
    for slot_index, offset in enumerate(neighbour_offsets):
        neighbour = nearby[2 + offset : 2 + offset + blocks]
        coupled_full = exact_einsum("bnm,bmp->bnp", coupling[:, slot_index], neighbour)
        coupled_term = exact_einsum("bnp,pr->bnr", coupled_full, sketch[slot_index + 1])
        sources = sources + weights_mask[:, slot_index, None, None] * coupled_term
    all_sources = lax.all_gather(sources, "grp", axis=1, tiled=True)
    sketched = exact_einsum("bnp,pr->bnr", primary, sketch[0]) - exact_einsum(
        "bnm,bmr->bnr", inverse_self, all_sources
    )
    gram_part = exact_einsum("bnr,bns->brs", sketched, sketched)
    gram_total = lax.psum(gram_part, "grp") / unknowns
    chol_lower = jnp.linalg.cholesky(gram_total)
    bases = lax.linalg.triangular_solve(
        chol_lower, sketched, left_side=False, lower=True, transpose_a=True
    )
    basis_shards = extended(bases, (("blk", 0),), 2)
    basis_near = lax.all_gather(basis_shards, "grp", axis=1, tiled=True)
    stacked = []
    for slot_index, offset in enumerate(neighbour_offsets):
        coupled_basis = exact_einsum(
            "bnm,bmr->bnr", coupling[:, slot_index], basis_near[2 + offset : 2 + offset + blocks]
        )
        stacked.append(exact_einsum("bnr,bns->brs", bases, coupled_basis))
    coupled_part = jnp.stack(stacked, axis=1)
    driven_part = exact_einsum("bnr,bnp->brp", bases, own_excitation)
    coupled_sum, driven_sum = lax.psum((coupled_part, driven_part), "grp")
    norm_scale = 1.0 / math.sqrt(unknowns)
    return (bases, coupled_sum * norm_scale, driven_sum * norm_scale)


def solution(mesh):
    return jax.shard_map(
        shards,
        mesh=mesh,
        in_specs=(
            P("blk", None, None),
            P("blk", "grp", None),
            P("blk", None, "grp", None),
            P("blk", None),
            P(),
        ),
        out_specs=(P("blk", "grp", None), P("blk", None, None, None), P("blk", None, None)),
        check_vma=False,
    )
```

profile of v0, /device:TPU:2, one launch (start us, length us, event | category | flops | bytes accessed | tf_op | source)
XLA Modules:
  0.0 315.8 jit_solution(14222659182359712413)
XLA Ops:
  7.2 0.0 copy-start
  7.2 0.0 all-gather.2.cloned.1.call-start
  7.3 1.1 copy-done
  8.4 2.1 fusion.57
  10.5 0.0 all-gather.2.cloned.1.call-update
  10.5 0.0 all-reduce.2.cloned.1.call-start
  10.5 46.6 %all-gather.2.cloned.1.call-done = f32[2,1024,256]{2,1,0:T(8,128)} async-done(((f32[2,128,256]{2,1,0:T(8,128)}), f32[2,1024,256]{2,1,0:T(8,128)}) %all-gather.2.cloned.1.call-update) | async-done | bytes 2097168 | tf_op jit(solution)/shard_map/all_gather | solution.py:39
  57.1 3.4 %collective-permute-start = (f32[2,1024,256]{2,1,0:T(8,128)}, f32[2,1024,256]{2,1,0:T(8,128)}, u32[]{:S(2)}, u32[]{:S(2)}) collective-permute-start(f32[2,1024,256]{2,1,0:T(8,128)} %all-gather.2.cloned.1.call-done), channel_id=1, source_target_pairs={{0,8},{8,16},{16,24},{24,32},{32,40},{40,48},{48,56},{56,64},{64,7... | collective-permute-start | bytes 6291464 | tf_op jit(solution)/shard_map/ppermute | solution.py:17
  60.5 9.4 %collective-permute-start.1 = (f32[2,1024,256]{2,1,0:T(8,128)}, f32[2,1024,256]{2,1,0:T(8,128)}, u32[]{:S(2)}, u32[]{:S(2)}) collective-permute-start(f32[2,1024,256]{2,1,0:T(8,128)} %all-gather.2.cloned.1.call-done), channel_id=1, source_target_pairs={{8,0},{16,8},{24,16},{32,24},{40,32},{48,40},{56,48},{64,56},{72,6... | collective-permute-start | bytes 6291464 | tf_op jit(solution)/shard_map/ppermute | solution.py:18
  70.0 0.2 slice_reduce_fusion
  70.2 1.4 fusion.47
  71.6 85.4 %collective-permute-done = f32[2,1024,256]{2,1,0:T(8,128)} collective-permute-done((f32[2,1024,256]{2,1,0:T(8,128)}, f32[2,1024,256]{2,1,0:T(8,128)}, u32[]{:S(2)}, u32[]{:S(2)}) %collective-permute-start) | collective-permute-done | bytes 2097184 | tf_op jit(solution)/shard_map/ppermute | solution.py:17
  157.0 3.4 %convolution_bitcast_fusion.1 = f32[2,128,256]{1,2,0:T(8,128)S(1)} fusion(f32[2,1024,256]{2,1,0:T(8,128)} %collective-permute-done, bf16[2,4,128,1024]{3,2,1,0:T(8,128)(2,1)S(1)} %copy-done.1), kind=kOutput, calls=%fused_computation.11 | convolution fusion | flops 805306368 | bytes 2883584 | tf_op jit(solution)/shard_map/bnm,bmp->bnp/dot_general | solution.py:24
  160.5 0.3 convolution_multiply_fusion.3
  160.8 3.0 fusion.11
  163.8 0.3 fusion.17
  164.1 3.0 fusion.8
  167.1 0.3 fusion.16
  167.4 3.4 %convolution_bitcast_fusion = f32[2,128,256]{1,2,0:T(8,128)S(1)} fusion(f32[2,1024,256]{2,1,0:T(8,128)} %collective-permute-done.1, bf16[2,4,128,1024]{3,2,1,0:T(8,128)(2,1)S(1)} %copy-done.1), kind=kOutput, calls=%fused_computation.10 | convolution fusion | flops 805306368 | bytes 2883584 | tf_op jit(solution)/shard_map/bnm,bmp->bnp/dot_general | solution.py:24
  170.8 0.3 fusion.15
  171.1 14.2 %all_gather.10 = f32[2,1024,32]{1,2,0:T(8,128)S(1)} all-gather(f32[2,128,32]{1,2,0:T(8,128)S(1)} %fusion.15), channel_id=1, replica_groups=mesh['blk'=64,'grp'=8] {'grp'}, dimensions={1}, use_global_device_ids=true | all-gather | bytes 294912 | tf_op jit(solution)/shard_map/all_gather | solution.py:47
  185.3 0.6 fusion.14
  185.9 0.2 fusion.58
  186.1 26.2 %psum.21 = f32[2,32,32]{1,2,0:T(8,128)S(1)} all-reduce(f32[2,32,32]{1,2,0:T(8,128)S(1)} %fusion.58), channel_id=1, replica_groups=mesh['blk'=64,'grp'=8] {'grp'}, use_global_device_ids=true, to_apply=%region_0.0 | all-reduce | flops 2048 | bytes 16384 | tf_op jit(solution)/shard_map/psum | solution.py:52
  212.3 0.1 copy.13
  212.4 5.9 %custom-call.7 = f32[2,32,32]{2,1,0:T(8,128)S(1)} custom-call(f32[2,32,32]{2,1,0:T(8,128)S(1)} %fusion.42), custom_call_target="Cholesky" | custom-call | tf_op jit(solution)/shard_map/jit(cholesky)/cholesky | solution.py:53
  218.3 0.1 compare_reduce_fusion
  218.4 0.1 select_bitcast_fusion
  218.5 4.9 %custom-call.8 = f32[2,1,32,32]{2,3,1,0:T(8,128)S(1)} custom-call(f32[2,1,32,32]{3,2,1,0:T(8,128)S(1)} %select_bitcast_fusion), custom_call_target="InvertDiagBlocksLowerTriangular" | custom-call | tf_op jit(solution)/shard_map/triangular_solve | solution.py:54
  223.4 0.3 fusion.40
  223.7 5.4 %collective-permute-start.3 = (f32[2,128,32]{1,2,0:T(8,128)S(1)}, f32[2,128,32]{1,2,0:T(8,128)S(1)}, u32[]{:S(2)}, u32[]{:S(2)}) collective-permute-start(f32[2,128,32]{1,2,0:T(8,128)S(1)} %fusion.40), channel_id=1, source_target_pairs={{8,0},{16,8},{24,16},{32,24},{40,32},{48,40},{56,48},{64,56},{72,6... | collective-permute-start | bytes 98312 | tf_op jit(solution)/shard_map/ppermute | solution.py:18
  229.1 1.9 collective-permute-start.2
  231.0 0.8 fusion.38
  231.9 0.0 all-reduce.2.cloned.1.call-update
  231.9 10.0 %collective-permute-done.2 = f32[2,128,32]{1,2,0:T(8,128)S(1)} collective-permute-done((f32[2,128,32]{1,2,0:T(8,128)S(1)}, f32[2,128,32]{1,2,0:T(8,128)S(1)}, u32[]{:S(2)}, u32[]{:S(2)}) %collective-permute-start.2) | collective-permute-done | bytes 32800 | tf_op jit(solution)/shard_map/ppermute | solution.py:17
  241.9 16.0 %all_gather.11 = f32[6,1024,32]{1,2,0:T(8,128)S(1)} all-gather(f32[6,128,32]{1,2,0:T(8,128)S(1)} %pad_maximum_fusion.1), channel_id=1, replica_groups=mesh['blk'=64,'grp'=8] {'grp'}, dimensions={1}, use_global_device_ids=true | all-gather | bytes 884736 | tf_op jit(solution)/shard_map/all_gather | solution.py:58
  257.9 0.6 fusion.18
  258.5 0.6 fusion.21
  259.1 0.6 fusion.24
  259.8 0.6 fusion.27
  260.4 0.2 convolution_bitcast_fusion.2
  260.6 0.2 convolution_bitcast_fusion.3
  260.7 0.2 convolution_bitcast_fusion.4
  260.9 0.2 convolution_bitcast_fusion.5
  261.1 27.9 %psum.22 = f32[2,4,32,32]{3,2,0,1:T(8,128)S(1)} all-reduce(f32[2,4,32,32]{3,2,0,1:T(8,128)S(1)} %pad_maximum_fusion), channel_id=1, replica_groups=mesh['blk'=64,'grp'=8] {'grp'}, use_global_device_ids=true, to_apply=%region_3.4 | all-reduce | flops 8192 | bytes 65536 | tf_op jit(solution)/shard_map/psum | solution.py:67
  289.1 0.7 copy.15
  289.7 17.8 %all-reduce.2.cloned.1.call-done = f32[2,32,256]{2,1,0:T(8,128)} async-done(((f32[2,32,256]{2,1,0:T(8,128)}), f32[2,32,256]{2,1,0:T(8,128)}) %all-reduce.2.cloned.1.call-update) | async-done | bytes 65552 | tf_op jit(solution)/shard_map/psum | solution.py:67
  307.5 1.5 broadcast_multiply_fusion.1
  (23 shorter events, 0.1 us)
Async XLA Ops:
  7.2 1.2 copy-start
  7.2 62.7 %copy-start.6 = (s32[2,4]{1,0:T(2,128)S(1)}, s32[2,4]{1,0:T(2,128)}, u32[]{:S(2)}) copy-start(s32[2,4]{1,0:T(2,128)} %param.8) | copy-start | bytes 100
  7.2 63.0 %copy-start.5 = (f32[5,256,32]{1,2,0:T(8,128)S(1)}, f32[5,256,32]{1,2,0:T(8,128)}, u32[]{:S(2)}) copy-start(f32[5,256,32]{1,2,0:T(8,128)} %param.9) | copy-start | bytes 491524
  7.2 149.8 %copy-start.1 = (bf16[2,4,128,1024]{3,2,1,0:T(8,128)(2,1)S(1)}, bf16[2,4,128,1024]{3,2,1,0:T(8,128)(2,1)}, u32[]{:S(2)}) copy-start(bf16[2,4,128,1024]{3,2,1,0:T(8,128)(2,1)} %param.7) | copy-start | bytes 6291460
  7.2 49.9 %all-gather.2.cloned.1.call-start = ((), (), s32[]{:S(2)}) async-start(), calls=%async_computation | async-start | bytes 2359296 | tf_op jit(solution)/shard_map/all_gather | solution.py:39
  10.5 297.0 %all-reduce.2.cloned.1.call-start = ((), (), s32[]{:S(2)}) async-start(), calls=%async_computation.1 | async-start | bytes 131072 | tf_op jit(solution)/shard_map/psum | solution.py:67
  57.1 99.9 %collective-permute-start = (f32[2,1024,256]{2,1,0:T(8,128)}, f32[2,1024,256]{2,1,0:T(8,128)}, u32[]{:S(2)}, u32[]{:S(2)}) collective-permute-start(f32[2,1024,256]{2,1,0:T(8,128)} %all-gather.2.cloned.1.call-done), channel_id=1, source_target_pairs={{0,8},{8,16},{16,24},{24,32},{32,40},{40,48},{48,56},{56,64},{64,7... | collective-permute-start | bytes 6291464 | tf_op jit(solution)/shard_map/ppermute | solution.py:17
  60.5 103.6 %collective-permute-start.1 = (f32[2,1024,256]{2,1,0:T(8,128)}, f32[2,1024,256]{2,1,0:T(8,128)}, u32[]{:S(2)}, u32[]{:S(2)}) collective-permute-start(f32[2,1024,256]{2,1,0:T(8,128)} %all-gather.2.cloned.1.call-done), channel_id=1, source_target_pairs={{8,0},{16,8},{24,16},{32,24},{40,32},{48,40},{56,48},{64,56},{72,6... | collective-permute-start | bytes 6291464 | tf_op jit(solution)/shard_map/ppermute | solution.py:18
  69.9 90.8 %copy-start.2 = (f32[2,1024,256]{2,1,0:T(8,128)S(1)}, f32[2,1024,256]{2,1,0:T(8,128)}, u32[]{:S(2)}) copy-start(f32[2,1024,256]{2,1,0:T(8,128)} %all-gather.2.cloned.1.call-done) | copy-start | bytes 6291460
  167.1 18.2 %copy-start.3 = (bf16[2,128,1024]{2,1,0:T(8,128)(2,1)S(1)}, bf16[2,128,1024]{2,1,0:T(8,128)(2,1)}, u32[]{:S(2)}) copy-start(bf16[2,128,1024]{2,1,0:T(8,128)(2,1)} %param.6) | copy-start | bytes 1572868
  223.7 37.2 %copy-start.4 = (f32[2,128,32]{1,2,0:T(8,128)}, f32[2,128,32]{1,2,0:T(8,128)S(1)}, u32[]{:S(2)}) copy-start(f32[2,128,32]{1,2,0:T(8,128)S(1)} %fusion.40) | copy-start | bytes 98308
  223.7 8.2 %collective-permute-start.3 = (f32[2,128,32]{1,2,0:T(8,128)S(1)}, f32[2,128,32]{1,2,0:T(8,128)S(1)}, u32[]{:S(2)}, u32[]{:S(2)}) collective-permute-start(f32[2,128,32]{1,2,0:T(8,128)S(1)} %fusion.40), channel_id=1, source_target_pairs={{8,0},{16,8},{24,16},{32,24},{40,32},{48,40},{56,48},{64,56},{72,6... | collective-permute-start | bytes 98312 | tf_op jit(solution)/shard_map/ppermute | solution.py:18
  229.1 12.8 %collective-permute-start.2 = (f32[2,128,32]{1,2,0:T(8,128)S(1)}, f32[2,128,32]{1,2,0:T(8,128)S(1)}, u32[]{:S(2)}, u32[]{:S(2)}) collective-permute-start(f32[2,128,32]{1,2,0:T(8,128)S(1)} %fusion.40), channel_id=1, source_target_pairs={{0,8},{8,16},{16,24},{24,32},{32,40},{40,48},{48,56},{56,64},{64,7... | collective-permute-start | bytes 98312 | tf_op jit(solution)/shard_map/ppermute | solution.py:17
Sparse Core Ops, SparseCore 0:
  10.6 46.4 all-gather.1
  232.0 75.4 all-reduce.1
where the time goes:
time: 316 us
  waiting for transfers between devices  160 us (51%)
  blocking collectives  84.3 us (27%)
  matrix products  22.4 us (7%)
  starting transfers between devices  20.1 us (6%)
  between operations  14.4 us (5%)
  other arithmetic  12.5 us (4%)
    ppermute x2, waiting for transfers between devices, extended(): before = lax.ppermute(last, axis, up)  95.5 us
    all_gather x1, waiting for transfers between devices, shards(): own_whole = lax.all_gather(primary, 'grp', axis=1, tiled=True)  46.6 us
    psum x1, blocking collectives, shards(): coupled_sum, driven_sum = lax.psum((coupled_part, driven_part), 'grp')  27.9 us
    psum x1, blocking collectives, shards(): gram_total = lax.psum(gram_part, 'grp') / unknowns  26.2 us
    dot_general x20, matrix products, exact_einsum(): jnp.einsum(form, left, right, precision=lax.Precision.HIGHEST, preferred_...  20.1 us
    psum x1, waiting for transfers between devices, shards(): coupled_sum, driven_sum = lax.psum((coupled_part, driven_part), 'grp')  17.8 us
    all_gather x1, blocking collectives, shards(): basis_near = lax.all_gather(basis_shards, 'grp', axis=1, tiled=True)  16 us
    ppermute x2, starting transfers between devices, extended(): after = lax.ppermute(initial, axis, down)  14.8 us
  transfers between devices with their start and end apart: 6, of which 4 were waited for; matrix products, arithmetic and copies ran while one was open for 4% of the time, Pallas kernels for 0%

commit v1 on v0

--- a/solution.py
+++ b/solution.py
@@ -36,7 +36,8 @@
         "bnm,bmp->bnp", inverse_self, excitation, preferred_element_type=jnp.float32
     )
     weights_mask = neighbour_mask.astype(jnp.float32)
-    own_whole = lax.all_gather(primary, "grp", axis=1, tiled=True)
+    sent = jnp.stack([primary] * lax.axis_size("grp"))
+    own_whole = jnp.concatenate(lax.all_to_all(sent, "grp", 0, 0), axis=1)
     nearby = extended(own_whole, (("blk", 0),), 2)
     sources = jnp.zeros((blocks, shard_rows, retained), jnp.float32)
     for slot_index, offset in enumerate(neighbour_offsets):

time: 316 us -> 331 us (1.047)
  blocking collectives: 84.3 us -> 143 us
  waiting for transfers between devices: 160 us -> 116 us
  matrix products: 22.4 us -> 18.6 us
  local copies, waits for them, and re-layouts: 2.13 us -> 5.8 us
    all_to_all x0 -> x1, blocking collectives: none -> 56.1 us  [shards(): own_whole = jnp.concatenate(lax.all_to_all(sent, 'grp', 0, 0), axis=1)]
    all_gather x1 -> x0, waiting for transfers between devices: 46.6 us -> none  [shards(): own_whole = lax.all_gather(primary, 'grp', axis=1, tiled=True)]
  transfers between devices with their start and end apart: 6 -> 5, of which waited for: 4 -> 3; matrix products, arithmetic and copies ran while one was open for 4% -> 4% of each run, Pallas kernels for 0% -> 0%
where the time goes in v1:
time: 331 us
  blocking collectives  143 us (43%)
  waiting for transfers between devices  116 us (35%)
  starting transfers between devices  20.5 us (6%)
  matrix products  18.6 us (6%)
  between operations  14.4 us (4%)
  other arithmetic  12.5 us (4%)
  local copies, waits for them, and re-layouts  5.8 us (2%)
    ppermute x2, waiting for transfers between devices, extended(): before = lax.ppermute(last, axis, up)  97.2 us
    all_to_all x1, blocking collectives, shards(): own_whole = jnp.concatenate(lax.all_to_all(sent, 'grp', 0, 0), axis=1)  56.1 us
    psum x1, blocking collectives, shards(): gram_total = lax.psum(gram_part, 'grp') / unknowns  29.1 us
    psum x1, blocking collectives, shards(): coupled_sum, driven_sum = lax.psum((coupled_part, driven_part), 'grp')  28 us
    psum x1, waiting for transfers between devices, shards(): coupled_sum, driven_sum = lax.psum((coupled_part, driven_part), 'grp')  18.3 us
    dot_general x20, matrix products, exact_einsum(): jnp.einsum(form, left, right, precision=lax.Precision.HIGHEST, preferred_...  17 us
    all_gather x1, blocking collectives, shards(): basis_near = lax.all_gather(basis_shards, 'grp', axis=1, tiled=True)  15.7 us
    ppermute x2, starting transfers between devices, extended(): after = lax.ppermute(initial, axis, down)  15 us
  transfers between devices with their start and end apart: 5, of which 3 were waited for; matrix products, arithmetic and copies ran while one was open for 4% of the time, Pallas kernels for 0%

profile of v1, /device:TPU:2, one launch (start us, length us, event | category | flops | bytes accessed | tf_op | source)
XLA Modules:
  0.0 330.7 jit_solution(14445957119212141808)
XLA Ops:
  7.2 0.0 all-reduce.2.cloned.1.call-start
  7.2 1.2 copy-done
  8.4 1.3 fusion.57
  9.7 0.2 stack.12
  9.9 56.1 %all_to_all.5 = f32[8,2,128,256]{3,2,1,0:T(8,128)S(1)} all-to-all(f32[8,2,128,256]{3,2,1,0:T(8,128)S(1)} %stack.12), channel_id=1, replica_groups=mesh['blk'=64,'grp'=8] {'grp'}, dimensions={0} | all-to-all | bytes 4194304 | tf_op jit(solution)/shard_map/all_to_all | solution.py:40
  66.0 1.5 copy.33
  67.5 1.9 copy.34
  69.5 3.5 %collective-permute-start = (f32[2,1024,256]{1,2,0:T(8,128)S(1)}, f32[2,1024,256]{1,2,0:T(8,128)}, u32[]{:S(2)}, u32[]{:S(2)}) collective-permute-start(f32[2,1024,256]{1,2,0:T(8,128)S(1)} %copy.34), channel_id=1, source_target_pairs={{0,8},{8,16},{16,24},{24,32},{32,40},{40,48},{48,56},{56,64},{64,7... | collective-permute-start | bytes 6291464 | tf_op jit(solution)/shard_map/ppermute | solution.py:17
  73.0 9.5 %collective-permute-start.1 = (f32[2,1024,256]{1,2,0:T(8,128)S(1)}, f32[2,1024,256]{1,2,0:T(8,128)}, u32[]{:S(2)}, u32[]{:S(2)}) collective-permute-start(f32[2,1024,256]{1,2,0:T(8,128)S(1)} %copy.34), channel_id=1, source_target_pairs={{8,0},{16,8},{24,16},{32,24},{40,32},{48,40},{56,48},{64,56},{72,6... | collective-permute-start | bytes 6291464 | tf_op jit(solution)/shard_map/ppermute | solution.py:18
  82.6 0.2 slice_reduce_fusion
  82.8 1.3 fusion.47
  84.1 87.3 %collective-permute-done = f32[2,1024,256]{1,2,0:T(8,128)} collective-permute-done((f32[2,1024,256]{1,2,0:T(8,128)S(1)}, f32[2,1024,256]{1,2,0:T(8,128)}, u32[]{:S(2)}, u32[]{:S(2)}) %collective-permute-start) | collective-permute-done | bytes 2097184 | tf_op jit(solution)/shard_map/ppermute | solution.py:17
  171.4 2.7 convolution_bitcast_fusion.1
  174.1 0.3 convolution_multiply_fusion.3
  174.4 2.3 fusion.11
  176.7 0.3 fusion.17
  177.0 2.3 fusion.8
  179.3 0.3 fusion.16
  179.5 2.7 convolution_bitcast_fusion
  182.2 0.3 fusion.15
  182.5 14.4 %all_gather.6 = f32[2,1024,32]{1,2,0:T(8,128)S(1)} all-gather(f32[2,128,32]{1,2,0:T(8,128)S(1)} %fusion.15), channel_id=1, replica_groups=mesh['blk'=64,'grp'=8] {'grp'}, dimensions={1}, use_global_device_ids=true | all-gather | bytes 294912 | tf_op jit(solution)/shard_map/all_gather | solution.py:48
  196.9 0.6 fusion.14
  197.5 0.2 fusion.58
  197.7 29.1 %psum.21 = f32[2,32,32]{1,2,0:T(8,128)S(1)} all-reduce(f32[2,32,32]{1,2,0:T(8,128)S(1)} %fusion.58), channel_id=1, replica_groups=mesh['blk'=64,'grp'=8] {'grp'}, use_global_device_ids=true, to_apply=%region_0.0 | all-reduce | flops 2048 | bytes 16384 | tf_op jit(solution)/shard_map/psum | solution.py:53
  226.8 0.1 copy.47
  226.9 5.9 %custom-call.7 = f32[2,32,32]{2,1,0:T(8,128)S(1)} custom-call(f32[2,32,32]{2,1,0:T(8,128)S(1)} %fusion.42), custom_call_target="Cholesky" | custom-call | tf_op jit(solution)/shard_map/jit(cholesky)/cholesky | solution.py:54
  232.8 0.1 compare_reduce_fusion
  232.9 0.1 select_bitcast_fusion
  233.0 4.9 %custom-call.8 = f32[2,1,32,32]{2,3,1,0:T(8,128)S(1)} custom-call(f32[2,1,32,32]{3,2,1,0:T(8,128)S(1)} %select_bitcast_fusion), custom_call_target="InvertDiagBlocksLowerTriangular" | custom-call | tf_op jit(solution)/shard_map/triangular_solve | solution.py:55
  237.9 0.3 fusion.40
  238.2 5.5 %collective-permute-start.3 = (f32[2,128,32]{1,2,0:T(8,128)S(1)}, f32[2,128,32]{1,2,0:T(8,128)S(1)}, u32[]{:S(2)}, u32[]{:S(2)}) collective-permute-start(f32[2,128,32]{1,2,0:T(8,128)S(1)} %fusion.40), channel_id=1, source_target_pairs={{8,0},{16,8},{24,16},{32,24},{40,32},{48,40},{56,48},{64,56},{72,6... | collective-permute-start | bytes 98312 | tf_op jit(solution)/shard_map/ppermute | solution.py:18
  243.7 1.9 collective-permute-start.2
  245.6 0.8 fusion.38
  246.4 0.0 all-reduce.2.cloned.1.call-update
  246.5 10.0 %collective-permute-done.2 = f32[2,128,32]{1,2,0:T(8,128)S(1)} collective-permute-done((f32[2,128,32]{1,2,0:T(8,128)S(1)}, f32[2,128,32]{1,2,0:T(8,128)S(1)}, u32[]{:S(2)}, u32[]{:S(2)}) %collective-permute-start.2) | collective-permute-done | bytes 32800 | tf_op jit(solution)/shard_map/ppermute | solution.py:17
  256.4 15.7 %all_gather.7 = f32[6,1024,32]{1,2,0:T(8,128)S(1)} all-gather(f32[6,128,32]{1,2,0:T(8,128)S(1)} %pad_maximum_fusion.1), channel_id=1, replica_groups=mesh['blk'=64,'grp'=8] {'grp'}, dimensions={1}, use_global_device_ids=true | all-gather | bytes 884736 | tf_op jit(solution)/shard_map/all_gather | solution.py:59
  272.2 0.6 fusion.18
  272.8 0.6 fusion.21
  273.4 0.6 fusion.24
  274.0 0.6 fusion.27
  274.6 0.2 convolution_bitcast_fusion.2
  274.8 0.2 convolution_bitcast_fusion.3
  275.0 0.2 convolution_bitcast_fusion.4
  275.2 0.2 convolution_bitcast_fusion.5
  275.4 28.0 %psum.22 = f32[2,4,32,32]{3,2,0,1:T(8,128)S(1)} all-reduce(f32[2,4,32,32]{3,2,0,1:T(8,128)S(1)} %pad_maximum_fusion), channel_id=1, replica_groups=mesh['blk'=64,'grp'=8] {'grp'}, use_global_device_ids=true, to_apply=%region_3.4 | all-reduce | flops 8192 | bytes 65536 | tf_op jit(solution)/shard_map/psum | solution.py:68
  303.4 0.7 copy.49
  304.1 18.3 %all-reduce.2.cloned.1.call-done = f32[2,32,256]{2,1,0:T(8,128)} async-done(((f32[2,32,256]{2,1,0:T(8,128)}), f32[2,32,256]{2,1,0:T(8,128)}) %all-reduce.2.cloned.1.call-update) | async-done | bytes 65552 | tf_op jit(solution)/shard_map/psum | solution.py:68
  322.4 1.5 broadcast_multiply_fusion.1
  (24 shorter events, 0.1 us)
Async XLA Ops:
  7.2 1.2 copy-start
  7.2 315.2 %all-reduce.2.cloned.1.call-start = ((), (), s32[]{:S(2)}) async-start(), calls=%async_computation.1 | async-start | bytes 131072 | tf_op jit(solution)/shard_map/psum | solution.py:68
  67.5 15.0 %copy-start.6 = (s32[2,4]{1,0:T(2,128)S(1)}, s32[2,4]{1,0:T(2,128)}, u32[]{:S(2)}) copy-start(s32[2,4]{1,0:T(2,128)} %param.8) | copy-start | bytes 100
  69.5 101.9 %collective-permute-start = (f32[2,1024,256]{1,2,0:T(8,128)S(1)}, f32[2,1024,256]{1,2,0:T(8,128)}, u32[]{:S(2)}, u32[]{:S(2)}) collective-permute-start(f32[2,1024,256]{1,2,0:T(8,128)S(1)} %copy.34), channel_id=1, source_target_pairs={{0,8},{8,16},{16,24},{24,32},{32,40},{40,48},{48,56},{56,64},{64,7... | collective-permute-start | bytes 6291464 | tf_op jit(solution)/shard_map/ppermute | solution.py:17
  73.0 104.0 %collective-permute-start.1 = (f32[2,1024,256]{1,2,0:T(8,128)S(1)}, f32[2,1024,256]{1,2,0:T(8,128)}, u32[]{:S(2)}, u32[]{:S(2)}) collective-permute-start(f32[2,1024,256]{1,2,0:T(8,128)S(1)} %copy.34), channel_id=1, source_target_pairs={{8,0},{16,8},{24,16},{32,24},{40,32},{48,40},{56,48},{64,56},{72,6... | collective-permute-start | bytes 6291464 | tf_op jit(solution)/shard_map/ppermute | solution.py:18
  82.6 91.5 %copy-start.5 = (f32[5,256,32]{1,2,0:T(8,128)S(1)}, f32[5,256,32]{1,2,0:T(8,128)}, u32[]{:S(2)}) copy-start(f32[5,256,32]{1,2,0:T(8,128)} %param.9) | copy-start | bytes 491524
  82.6 91.8 %copy-start.1 = (bf16[2,4,128,1024]{3,2,1,0:T(8,128)(2,1)S(1)}, bf16[2,4,128,1024]{3,2,1,0:T(8,128)(2,1)}, u32[]{:S(2)}) copy-start(bf16[2,4,128,1024]{3,2,1,0:T(8,128)(2,1)} %param.7) | copy-start | bytes 6291460
  179.3 17.6 %copy-start.3 = (bf16[2,128,1024]{2,1,0:T(8,128)(2,1)S(1)}, bf16[2,128,1024]{2,1,0:T(8,128)(2,1)}, u32[]{:S(2)}) copy-start(bf16[2,128,1024]{2,1,0:T(8,128)(2,1)} %param.6) | copy-start | bytes 1572868
  182.2 90.0 %copy-start.2 = (bf16[2,4,128,1024]{3,2,1,0:T(8,128)(2,1)S(1)}, bf16[2,4,128,1024]{3,2,1,0:T(8,128)(2,1)}, u32[]{:S(2)}) copy-start(bf16[2,4,128,1024]{3,2,1,0:T(8,128)(2,1)} %param.7) | copy-start | bytes 6291460
  238.2 37.0 %copy-start.4 = (f32[2,128,32]{1,2,0:T(8,128)}, f32[2,128,32]{1,2,0:T(8,128)S(1)}, u32[]{:S(2)}) copy-start(f32[2,128,32]{1,2,0:T(8,128)S(1)} %fusion.40) | copy-start | bytes 98308
  238.2 8.3 %collective-permute-start.3 = (f32[2,128,32]{1,2,0:T(8,128)S(1)}, f32[2,128,32]{1,2,0:T(8,128)S(1)}, u32[]{:S(2)}, u32[]{:S(2)}) collective-permute-start(f32[2,128,32]{1,2,0:T(8,128)S(1)} %fusion.40), channel_id=1, source_target_pairs={{8,0},{16,8},{24,16},{32,24},{40,32},{48,40},{56,48},{64,56},{72,6... | collective-permute-start | bytes 98312 | tf_op jit(solution)/shard_map/ppermute | solution.py:18
  243.7 12.7 %collective-permute-start.2 = (f32[2,128,32]{1,2,0:T(8,128)S(1)}, f32[2,128,32]{1,2,0:T(8,128)S(1)}, u32[]{:S(2)}, u32[]{:S(2)}) collective-permute-start(f32[2,128,32]{1,2,0:T(8,128)S(1)} %fusion.40), channel_id=1, source_target_pairs={{0,8},{8,16},{16,24},{24,32},{32,40},{40,48},{48,56},{56,64},{64,7... | collective-permute-start | bytes 98312 | tf_op jit(solution)/shard_map/ppermute | solution.py:17
Sparse Core Ops, SparseCore 0:
  246.6 75.7 all-reduce.1
